TPU v7x, 256 devices: a whole 4x4x8 slice. The times are simulated.
256 devices in a mesh: section: 8 (over y, core), dp: 32 (over z, x).
Axes of the slice: x: 4, y: 4, z: 8, core: 2. Of those that a mesh axis runs over, the one named last changes fastest.
Arguments:
- crop_maps: bfloat16 [32, 4, 2, 8, 8, 640], P('dp'), may hold values from -6 to 6
- target_maps: int32 [32, 4, 2, 8, 8], P('dp'), may hold values 0 or 1
- crop_counts: int32 [32, 4], P('dp'), may hold values from 1 to 2, as said below
- depth_kernels: float32 [8, 49, 640], P('section'), may hold values from -0.875 to 0.875
- weight_in: bfloat16 [8, 640, 2560], P('section', 'dp'), may hold values from -0.25 to 0.25
- weight_out: bfloat16 [8, 2560, 640], P('section', 'dp'), may hold values from -0.125 to 0.125
- head_weight: float32 [640], replicated, may hold values from -0.25 to 0.25
Outputs:
- grad_in: float32 [8, 640, 2560], P('section', 'dp')
- grad_out: float32 [8, 2560, 640], P('section', 'dp')
- grad_kernels: float32 [8, 49, 640], P('section')
- grad_head: float32 [640], replicated
- loss_value: float32 [], replicated
Inputs may be any that keep to these rules, and one draw needn't show every extreme that they name: `crop_counts`: every data group has some micro-batch with exactly 2 crops.
All inputs are finite; a program needn't handle non-finite values. No bound on the sum of `target_maps` on one device may be relied on, other than what follows from the above.
Results may differ from a plain program's by a relative error of at most 0.034.
Values may be sent and summed in bfloat16 or wider, within the bound.
No kernel may reach another device: no remote copies, remote signals or barrier semaphores. Data moves between devices by JAX's collectives and lax.ppermute only.
A program may use at most 128 MiB of HBM per device.

v0:
```python
import jax
import jax.numpy as jnp
from jax import lax
from jax.sharding import PartitionSpec as P

EPSILON = 1e-06
SQRT_HALF = 0.7071067811865476
INV_ROOT_TWO_PI = 0.3989422804014327


def from_behind(value, axis, steps):
    count = lax.axis_size(axis)
    first, last = (max(0, -steps), min(count, count - steps))
    return lax.ppermute(value, axis, [(source, source + steps) for source in range(first, last)])


def depthwise(values, kernel):
    side = values.shape[1]
    padded = jnp.pad(values, ((0, 0), (3, 3), (3, 3), (0, 0)))
    result = jnp.zeros_like(values)
    for vertical in range(7):
        for across in range(7):
            result = (
                result
                + padded[:, vertical : vertical + side, across : across + side, :]
                * kernel[vertical * 7 + across]
            )
    return result


def depthwise_back(grads, kernel):
    side = grads.shape[1]
    padded = jnp.pad(grads, ((0, 0), (3, 3), (3, 3), (0, 0)))
    result = jnp.zeros_like(grads)
    for vertical in range(7):
        for across in range(7):
            result = (
                result
                + padded[:, 6 - vertical : 6 - vertical + side, 6 - across : 6 - across + side, :]
                * kernel[vertical * 7 + across]
            )
    return result


def kernel_grad(values, grads):
    side = values.shape[1]
    padded = jnp.pad(values, ((0, 0), (3, 3), (3, 3), (0, 0)))
    taps = []
    for vertical in range(7):
        for across in range(7):
            taps.append(
                jnp.sum(
                    padded[:, vertical : vertical + side, across : across + side, :] * grads,
                    axis=(0, 1, 2),
                )
            )
    return jnp.stack(taps, axis=0)


def block_parts(tiles, kernel, weight_in):
    width = tiles.shape[-1]
    widened = tiles.astype(jnp.float32)
    mixed = depthwise(widened, kernel).reshape(-1, width)
    centred = mixed - jnp.mean(mixed, axis=-1, keepdims=True)
    inverse = lax.rsqrt(jnp.mean(centred * centred, axis=-1, keepdims=True) + EPSILON)
    normed = centred * inverse
    normed_low = normed.astype(jnp.bfloat16)
    hidden = jnp.dot(normed_low, weight_in, preferred_element_type=jnp.float32)
    activated = (hidden * 0.5 * (1.0 + lax.erf(hidden * SQRT_HALF))).astype(jnp.bfloat16)
    return (widened, normed, inverse, normed_low, hidden, activated)


def block_forward(tiles, kernel, weight_in, weight_out):
    width = tiles.shape[-1]
    widened, normed, inverse, normed_low, hidden, activated = block_parts(tiles, kernel, weight_in)
    output = jnp.dot(activated, weight_out, preferred_element_type=jnp.float32)
    return (widened.reshape(-1, width) + output).astype(jnp.bfloat16).reshape(tiles.shape)


def block_backward(tiles, upstream, kernel, weight_in, weight_out):
    width = tiles.shape[-1]
    widened, normed, inverse, normed_low, hidden, activated = block_parts(tiles, kernel, weight_in)
    up_flat = upstream.reshape(-1, width)
    through = lax.dot_general(
        up_flat, weight_out, (((1,), (1,)), ((), ())), preferred_element_type=jnp.float32
    )
    slope = (
        0.5 * (1.0 + lax.erf(hidden * SQRT_HALF))
        + hidden * jnp.exp(-0.5 * hidden * hidden) * INV_ROOT_TWO_PI
    )
    hidden_grad = (through * slope).astype(jnp.bfloat16)
    normed_grad = lax.dot_general(
        hidden_grad, weight_in, (((1,), (1,)), ((), ())), preferred_element_type=jnp.float32
    )
    mixed_grad = inverse * (
        normed_grad
        - jnp.mean(normed_grad, axis=-1, keepdims=True)
        - normed * jnp.mean(normed_grad * normed, axis=-1, keepdims=True)
    )
    mixed_tiles = mixed_grad.reshape(tiles.shape)
    kernel_term = kernel_grad(widened, mixed_tiles)
    tile_grad = (upstream.astype(jnp.float32) + depthwise_back(mixed_tiles, kernel)).astype(
        jnp.bfloat16
    )
    return (tile_grad, kernel_term, normed_low, hidden_grad, activated, up_flat)


def outer_sum(left, right):
    return lax.dot_general(
        left, right, (((0,), (0,)), ((), ())), preferred_element_type=jnp.float32
    )


def head_terms(final, targets, live, head_weight, factor):
    widened = final.astype(jnp.float32)
    logits = jnp.sum(widened * head_weight, axis=-1)
    weight_live = live.astype(jnp.float32)[:, :, None, None]
    truth = targets.astype(jnp.float32)
    loss_term = jnp.sum(weight_live * (jax.nn.softplus(logits) - truth * logits)) * factor
    logit_grad = (jax.nn.sigmoid(logits) - truth) * weight_live * factor
    seeds = (logit_grad[..., None] * head_weight).astype(jnp.bfloat16)
    head_term = jnp.sum(logit_grad[..., None] * widened, axis=(0, 1, 2, 3))
    return (loss_term, seeds, head_term)


def body(crop_maps, target_maps, crop_counts, depth_kernels, weight_in, weight_out, head_weight):
    section_index = lax.axis_index("section")
    section_count = lax.axis_size("section")
    micro_count = crop_maps.shape[1]
    slot_count = crop_maps.shape[2]
    kernel = depth_kernels[0]
    live = jnp.arange(slot_count)[None, :] < crop_counts[0][:, None]
    entering = crop_maps[0] * live[:, :, None, None, None].astype(jnp.bfloat16)
    first_full, second_full = (
        lax.all_gather(weight_in[0], "dp", axis=0, tiled=True),
        lax.all_gather(weight_out[0], "dp", axis=0, tiled=True),
    )
    blank_tile = jnp.zeros(entering.shape[1:], jnp.bfloat16)
    ticks = micro_count + section_count - 1

    def forward_step(moment, carry):
        arrived, saved, final = carry
        micro = moment - section_index
        active = (micro >= 0) & (micro < micro_count)
        place = jnp.clip(micro, 0, micro_count - 1)
        own_tiles = lax.dynamic_index_in_dim(entering, place, 0, keepdims=False)
        current = jnp.where(section_index == 0, own_tiles, arrived)
        result = lax.cond(
            active,
            lambda tiles: block_forward(tiles, kernel, first_full, second_full),
            lambda tiles: jnp.zeros_like(tiles),
            current,
        )
        old_saved = lax.dynamic_index_in_dim(saved, place, 0, keepdims=False)
        saved = lax.dynamic_update_index_in_dim(
            saved, jnp.where(active, current, old_saved), place, 0
        )
        old_final = lax.dynamic_index_in_dim(final, place, 0, keepdims=False)
        final = lax.dynamic_update_index_in_dim(
            final, jnp.where(active, result, old_final), place, 0
        )
        arrived = from_behind(result, "section", 1)
        return (arrived, saved, final)

    _, saved, final = lax.fori_loop(
        0, ticks, forward_step, (blank_tile, jnp.zeros_like(entering), jnp.zeros_like(entering))
    )
    is_last = section_index == section_count - 1
    last_weight = is_last.astype(jnp.float32)
    factor = 1.0 / (micro_count * slot_count)
    loss_term, seeds, head_term = head_terms(final, target_maps[0], live, head_weight, factor)
    head_total, loss_total = lax.psum(
        (head_term * last_weight, loss_term * last_weight), ("section", "dp")
    )
    first_back, second_back = (
        lax.all_gather(weight_in[0], "dp", axis=0, tiled=True),
        lax.all_gather(weight_out[0], "dp", axis=0, tiled=True),
    )
    width = entering.shape[-1]
    expand = first_back.shape[1]
    extra_start = (jnp.zeros((width, expand), jnp.float32), jnp.zeros((expand, width), jnp.float32))

    def backward_step(moment, carry):
        arrived, kernel_acc, extra = carry
        micro = moment - (section_count - 1 - section_index)
        active = (micro >= 0) & (micro < micro_count)
        place = jnp.clip(micro, 0, micro_count - 1)
        own_seed = lax.dynamic_index_in_dim(seeds, place, 0, keepdims=False)
        upstream = jnp.where(is_last, own_seed, arrived)
        stored = lax.dynamic_index_in_dim(saved, place, 0, keepdims=False)

        def run_block(operands):
            grad_tiles, inputs, acc_kernel, acc_extra = operands
            tile_grad, kernel_term, normed_low, hidden_grad, activated, up_flat = block_backward(
                inputs, grad_tiles, kernel, first_back, second_back
            )
            new_extra = (
                acc_extra[0] + outer_sum(normed_low, hidden_grad),
                acc_extra[1] + outer_sum(activated, up_flat),
            )
            return (tile_grad, acc_kernel + kernel_term, new_extra)

        def skip_block(operands):
            return (jnp.zeros_like(operands[0]), operands[2], operands[3])

        tile_grad, kernel_acc, extra = lax.cond(
            active, run_block, skip_block, (upstream, stored, kernel_acc, extra)
        )
        arrived = from_behind(tile_grad, "section", -1)
        return (arrived, kernel_acc, extra)

    _, kernel_acc, extra = lax.fori_loop(
        0, ticks, backward_step, (blank_tile, jnp.zeros(kernel.shape, jnp.float32), extra_start)
    )
    first_part, second_part = (
        lax.psum_scatter(
            extra[0].astype(jnp.bfloat16), "dp", scatter_dimension=0, tiled=True
        ).astype(jnp.float32),
        lax.psum_scatter(
            extra[1].astype(jnp.bfloat16), "dp", scatter_dimension=0, tiled=True
        ).astype(jnp.float32),
    )
    kernel_total = lax.psum(kernel_acc.astype(jnp.bfloat16), "dp").astype(jnp.float32)
    return (first_part[None], second_part[None], kernel_total[None], head_total, loss_total)


def solution(mesh):
    return jax.shard_map(
        body,
        mesh=mesh,
        in_specs=(
            P("dp", None, None, None, None, None),
            P("dp", None, None, None, None),
            P("dp", None),
            P("section", None, None),
            P("section", "dp", None),
            P("section", "dp", None),
            P(),
        ),
        out_specs=(
            P("section", "dp", None),
            P("section", "dp", None),
            P("section", None, None),
            P(),
            P(),
        ),
        check_vma=False,
    )
```

profile of v0, /device:TPU:1, one launch (start us, length us, event | category | flops | bytes accessed | tf_op | source)
XLA Modules:
  0.0 1533.0 jit_solution(5656709828315738469)
XLA Ops:
  13.1 91.3 %all-gather.5.cloned.1.call-done = bf16[1,640,2560]{2,0,1:T(2,128)(2,1)} async-done(((bf16[1,20,2560]{2,0,1:T(2,128)(2,1)}), bf16[1,640,2560]{2,0,1:T(2,128)(2,1)}) %all-gather.5.cloned.1.call-update) | async-done | bytes 3276816 | tf_op jit(solution)/shard_map/all_gather | solution.py:135
  104.4 3.6 copy.20
  108.0 72.7 %all-gather.7.cloned.1.call-done = bf16[1,2560,640]{2,1,0:T(8,128)(2,1)} async-done(((bf16[1,80,640]{2,1,0:T(8,128)(2,1)}), bf16[1,2560,640]{2,1,0:T(8,128)(2,1)}) %all-gather.7.cloned.1.call-update) | async-done | bytes 3276816 | tf_op jit(solution)/shard_map/all_gather | solution.py:136
  183.2 210.7 %while.40 = (s32[]{:T(128)}, bf16[2,8,8,640]{3,2,1,0:T(8,128)(2,1)}, bf16[4,2,8,8,640]{4,3,2,1,0:T(8,128)(2,1)}, bf16[4,2,8,8,640]{4,3,2,1,0:T(8,128)(2,1)}, s32...) while((s32[]{:T(128)}, ...), condition=%wide.region_5.6_spmd, body=%wide.region_0.5_spmd.sunk | while | flops 849510528 | bytes 13491009 | solution.py:165
  185.9 7.7 collective-permute-start
  195.4 12.2 collective-permute-done
  210.3 14.7 conditional.5
  231.9 14.7 conditional.5
  246.6 4.5 collective-permute-start
  256.1 14.7 conditional.5
  270.8 4.5 collective-permute-start
  280.3 14.7 conditional.5
  295.0 4.5 collective-permute-start
  304.5 19.2 %collective-permute-start = (bf16[2,8,8,640]{3,2,1,0:T(8,128)(2,1)S(1)}, bf16[2,8,8,640]{3,2,1,0:T(8,128)(2,1)}, u32[]{:S(2)}, u32[]{:S(2)}) collective-permute-start(bf16[2,8,8,640]{3,2,1,0:T(8,128)(2,1)S(1)} %get-tuple-element.1153), channel_id=1, source_target_pairs={{0,32},{32,64},{64,96},{96,128},{128,160},{160,192},{192,224},{1,3... | collective-permute-start | bytes 491528 | tf_op jit(solution)/shard_map/while/body/eval_jaxpr/ppermute | solution.py:14
  328.7 4.5 collective-permute-start
  338.2 12.7 collective-permute-start
  355.9 4.5 collective-permute-start
  365.5 16.6 %collective-permute-start = (bf16[2,8,8,640]{3,2,1,0:T(8,128)(2,1)S(1)}, bf16[2,8,8,640]{3,2,1,0:T(8,128)(2,1)}, u32[]{:S(2)}, u32[]{:S(2)}) collective-permute-start(bf16[2,8,8,640]{3,2,1,0:T(8,128)(2,1)S(1)} %get-tuple-element.1153), channel_id=1, source_target_pairs={{0,32},{32,64},{64,96},{96,128},{128,160},{160,192},{192,224},{1,3... | collective-permute-start | bytes 491528 | tf_op jit(solution)/shard_map/while/body/eval_jaxpr/ppermute | solution.py:14
  387.1 4.5 collective-permute-start
  403.2 778.2 %while.41 = (s32[]{:T(128)}, bf16[2,8,8,640]{3,2,1,0:T(8,128)(2,1)}, f32[49,640]{1,0:T(8,128)S(1)}, f32[640,2560]{1,0:T(8,128)}, f32[2560,640]{1,0:T(8,128)}, /*...) while((s32[]{:T(128)}, ...), condition=%wide.region_63.64_spmd.clone, body=%wide.region_7.63_spmd.clone.sunk | while | flops 2131804288 | bytes 130983528 | solution.py:212
  407.5 14.1 collective-permute-done.1
  425.9 5.0 collective-permute-done.1
  435.2 17.3 %collective-permute-done.1 = bf16[2,8,8,640]{3,2,1,0:T(8,128)(2,1)} collective-permute-done((bf16[2,8,8,640]{3,2,1,0:T(8,128)(2,1)}, bf16[2,8,8,640]{3,2,1,0:T(8,128)(2,1)}, u32[]{:S(2)}, u32[]{:S(2)}) %collective-permute-start.1) | collective-permute-done | bytes 163872 | tf_op jit(solution)/shard_map/while/body/eval_jaxpr/ppermute | solution.py:14
  456.8 5.0 collective-permute-done.1
  466.1 13.4 collective-permute-done.1
  483.8 359.0 %collective-permute-done.1 = bf16[2,8,8,640]{3,2,1,0:T(8,128)(2,1)} collective-permute-done((bf16[2,8,8,640]{3,2,1,0:T(8,128)(2,1)}, bf16[2,8,8,640]{3,2,1,0:T(8,128)(2,1)}, u32[]{:S(2)}, u32[]{:S(2)}) %collective-permute-start.1) | collective-permute-done | bytes 163872 | tf_op jit(solution)/shard_map/while/body/eval_jaxpr/ppermute | solution.py:14
  844.6 60.5 %conditional.6 = (bf16[2,8,8,640]{3,2,1,0:T(8,128)(2,1)}, f32[49,640]{1,0:T(8,128)S(1)}, f32[640,2560]{1,0:T(8,128)}, f32[2560,640]{1,0:T(8,128)}) conditional(s32[]{:T(128)} %convert_element_type.175, (f32[49,640]{1,0:T(8,128)S(1)}, f32[640,2560]{1,0:T(8,128)}, f32[2560,640]{1,0:T(8,128)}) %tuple.251, (pred[]{:T(512)}, s32[]{:T(128)}, ...), branch_computations={%region_8.8_spmd, %region_9.62_spmd} | conditional | flops 2131148928 | bytes 129667864 | solution.py:206
  884.0 8.0 stack.299
  893.8 7.2 convolution_add_fusion.1
  906.9 5.0 collective-permute-done.1
  913.7 60.5 %conditional.6 = (bf16[2,8,8,640]{3,2,1,0:T(8,128)(2,1)}, f32[49,640]{1,0:T(8,128)S(1)}, f32[640,2560]{1,0:T(8,128)}, f32[2560,640]{1,0:T(8,128)}) conditional(s32[]{:T(128)} %convert_element_type.175, (f32[49,640]{1,0:T(8,128)S(1)}, f32[640,2560]{1,0:T(8,128)}, f32[2560,640]{1,0:T(8,128)}) %tuple.251, (pred[]{:T(512)}, s32[]{:T(128)}, ...), branch_computations={%region_8.8_spmd, %region_9.62_spmd} | conditional | flops 2131148928 | bytes 129667864 | solution.py:206
  953.1 8.0 stack.299
  962.9 7.2 convolution_add_fusion.1
  976.0 5.0 collective-permute-done.1
  982.8 60.5 %conditional.6 = (bf16[2,8,8,640]{3,2,1,0:T(8,128)(2,1)}, f32[49,640]{1,0:T(8,128)S(1)}, f32[640,2560]{1,0:T(8,128)}, f32[2560,640]{1,0:T(8,128)}) conditional(s32[]{:T(128)} %convert_element_type.175, (f32[49,640]{1,0:T(8,128)S(1)}, f32[640,2560]{1,0:T(8,128)}, f32[2560,640]{1,0:T(8,128)}) %tuple.251, (pred[]{:T(512)}, s32[]{:T(128)}, ...), branch_computations={%region_8.8_spmd, %region_9.62_spmd} | conditional | flops 2131148928 | bytes 129667864 | solution.py:206
  1022.2 8.0 stack.299
  1032.0 7.2 convolution_add_fusion.1
  1045.1 5.0 collective-permute-done.1
  1051.9 60.5 %conditional.6 = (bf16[2,8,8,640]{3,2,1,0:T(8,128)(2,1)}, f32[49,640]{1,0:T(8,128)S(1)}, f32[640,2560]{1,0:T(8,128)}, f32[2560,640]{1,0:T(8,128)}) conditional(s32[]{:T(128)} %convert_element_type.175, (f32[49,640]{1,0:T(8,128)S(1)}, f32[640,2560]{1,0:T(8,128)}, f32[2560,640]{1,0:T(8,128)}) %tuple.251, (pred[]{:T(512)}, s32[]{:T(128)}, ...), branch_computations={%region_8.8_spmd, %region_9.62_spmd} | conditional | flops 2131148928 | bytes 129667864 | solution.py:206
  1091.3 8.0 stack.299
  1101.1 7.2 convolution_add_fusion.1
  1114.2 5.0 collective-permute-done.1
  1121.6 58.4 %collective-permute-start.1 = (bf16[2,8,8,640]{3,2,1,0:T(8,128)(2,1)}, bf16[2,8,8,640]{3,2,1,0:T(8,128)(2,1)}, u32[]{:S(2)}, u32[]{:S(2)}) collective-permute-start(bf16[2,8,8,640]{3,2,1,0:T(8,128)(2,1)} %get-tuple-element.1051), channel_id=1, source_target_pairs={{32,0},{64,32},{96,64},{128,96},{160,128},{192,160},{224,192},{33,... | collective-permute-start | bytes 491528 | tf_op jit(solution)/shard_map/while/body/eval_jaxpr/ppermute | solution.py:14
  1181.3 4.9 convert_element_type.134
  1191.4 84.2 %fusion.2 = bf16[24,2560]{1,0:T(8,128)(2,1)} fusion(bf16[640,2560]{1,0:T(8,128)(2,1)S(1)} %convert_element_type.133), kind=kCustom, calls=%all-reduce-scatter | all-reduce-scatter fusion | flops 1966081 | bytes 3400704
  1283.4 9.5 collective-permute-start.7
  1294.3 110.5 %psum.21 = bf16[1,49,640]{2,0,1:T(2,128)(2,1)S(1)} all-reduce(bf16[1,49,640]{2,0,1:T(2,128)(2,1)S(1)} %broadcast_in_dim.64), channel_id=1, replica_groups=mesh['section'=8,'dp'=32] {'dp'}, use_global_device_ids=true, to_apply=%region_66.67 | all-reduce | flops 31360 | bytes 125440 | tf_op jit(solution)/shard_map/psum | solution.py:223
  1406.9 115.7 %all-reduce.5 = (f32[640]{0:T(1024)}, f32[]{:T(128)}) all-reduce(f32[640]{0:T(1024)S(1)} %broadcast_multiply_fusion.4, f32[]{:T(128)S(6)} %mul.2377), channel_id=1, replica_groups=mesh['section'=8,'dp'=32] {'section','dp'}, use_global_device_ids=true, to_apply=%region_68.69 | all-reduce | flops 641 | bytes 5128 | tf_op jit(solution)/shard_map/psum | solution.py:172
  (1152 shorter events, 376.4 us)
Async XLA Ops:
  7.2 97.2 %all-gather.5.cloned.1.call-start = ((), (), s32[]{:S(2)}) async-start(), calls=%async_computation.2 | async-start | bytes 6758400 | tf_op jit(solution)/shard_map/all_gather | solution.py:135
  9.0 171.6 %all-gather.7.cloned.1.call-start = ((), (), s32[]{:S(2)}) async-start(), calls=%async_computation.3 | async-start | bytes 3379200 | tf_op jit(solution)/shard_map/all_gather | solution.py:136
  9.8 1515.1 %reduce-scatter.4.cloned.1.call-start = ((), (), s32[]{:S(2)}) async-start(), calls=%async_computation.1 | async-start | bytes 3379200 | tf_op jit(solution)/shard_map/reduce_scatter | solution.py:219
  183.2 212.0 %copy-start.81 = (s32[1,4,2,8,8]{4,3,2,1,0:T(8,128)S(1)}, s32[1,4,2,8,8]{4,3,2,1,0:T(8,128)}, u32[]{:S(2)}) copy-start(s32[1,4,2,8,8]{4,3,2,1,0:T(8,128)} %param.16) | copy-start | bytes 6148
  185.9 21.6 %collective-permute-start = (bf16[2,8,8,640]{3,2,1,0:T(8,128)(2,1)S(1)}, bf16[2,8,8,640]{3,2,1,0:T(8,128)(2,1)}, u32[]{:S(2)}, u32[]{:S(2)}) collective-permute-start(bf16[2,8,8,640]{3,2,1,0:T(8,128)(2,1)S(1)} %get-tuple-element.1153), channel_id=1, source_target_pairs={{0,32},{32,64},{64,96},{96,128},{128,160},{160,192},{192,224},{1,3... | collective-permute-start | bytes 491528 | tf_op jit(solution)/shard_map/while/body/eval_jaxpr/ppermute | solution.py:14
  225.0 4.2 collective-permute-start
  246.6 6.8 collective-permute-start
  270.8 6.7 collective-permute-start
  295.0 6.7 collective-permute-start
  304.5 21.4 %collective-permute-start = (bf16[2,8,8,640]{3,2,1,0:T(8,128)(2,1)S(1)}, bf16[2,8,8,640]{3,2,1,0:T(8,128)(2,1)}, u32[]{:S(2)}, u32[]{:S(2)}) collective-permute-start(bf16[2,8,8,640]{3,2,1,0:T(8,128)(2,1)S(1)} %get-tuple-element.1153), channel_id=1, source_target_pairs={{0,32},{32,64},{64,96},{96,128},{128,160},{160,192},{192,224},{1,3... | collective-permute-start | bytes 491528 | tf_op jit(solution)/shard_map/while/body/eval_jaxpr/ppermute | solution.py:14
  328.7 6.7 collective-permute-start
  338.2 14.9 collective-permute-start
  355.9 6.7 collective-permute-start
  365.5 18.8 %collective-permute-start = (bf16[2,8,8,640]{3,2,1,0:T(8,128)(2,1)S(1)}, bf16[2,8,8,640]{3,2,1,0:T(8,128)(2,1)}, u32[]{:S(2)}, u32[]{:S(2)}) collective-permute-start(bf16[2,8,8,640]{3,2,1,0:T(8,128)(2,1)S(1)} %get-tuple-element.1153), channel_id=1, source_target_pairs={{0,32},{32,64},{64,96},{96,128},{128,160},{160,192},{192,224},{1,3... | collective-permute-start | bytes 491528 | tf_op jit(solution)/shard_map/while/body/eval_jaxpr/ppermute | solution.py:14
  387.1 6.7 collective-permute-start
  405.6 16.0 %collective-permute-start.1 = (bf16[2,8,8,640]{3,2,1,0:T(8,128)(2,1)}, bf16[2,8,8,640]{3,2,1,0:T(8,128)(2,1)}, u32[]{:S(2)}, u32[]{:S(2)}) collective-permute-start(bf16[2,8,8,640]{3,2,1,0:T(8,128)(2,1)} %get-tuple-element.1051), channel_id=1, source_target_pairs={{32,0},{64,32},{96,64},{128,96},{160,128},{192,160},{224,192},{33,... | collective-permute-start | bytes 491528 | tf_op jit(solution)/shard_map/while/body/eval_jaxpr/ppermute | solution.py:14
  423.9 6.9 collective-permute-start.1
  433.3 19.2 %collective-permute-start.1 = (bf16[2,8,8,640]{3,2,1,0:T(8,128)(2,1)}, bf16[2,8,8,640]{3,2,1,0:T(8,128)(2,1)}, u32[]{:S(2)}, u32[]{:S(2)}) collective-permute-start(bf16[2,8,8,640]{3,2,1,0:T(8,128)(2,1)} %get-tuple-element.1051), channel_id=1, source_target_pairs={{32,0},{64,32},{96,64},{128,96},{160,128},{192,160},{224,192},{33,... | collective-permute-start | bytes 491528 | tf_op jit(solution)/shard_map/while/body/eval_jaxpr/ppermute | solution.py:14
  454.9 6.9 collective-permute-start.1
  464.2 15.3 %collective-permute-start.1 = (bf16[2,8,8,640]{3,2,1,0:T(8,128)(2,1)}, bf16[2,8,8,640]{3,2,1,0:T(8,128)(2,1)}, u32[]{:S(2)}, u32[]{:S(2)}) collective-permute-start(bf16[2,8,8,640]{3,2,1,0:T(8,128)(2,1)} %get-tuple-element.1051), channel_id=1, source_target_pairs={{32,0},{64,32},{96,64},{128,96},{160,128},{192,160},{224,192},{33,... | collective-permute-start | bytes 491528 | tf_op jit(solution)/shard_map/while/body/eval_jaxpr/ppermute | solution.py:14
  481.9 361.0 %collective-permute-start.1 = (bf16[2,8,8,640]{3,2,1,0:T(8,128)(2,1)}, bf16[2,8,8,640]{3,2,1,0:T(8,128)(2,1)}, u32[]{:S(2)}, u32[]{:S(2)}) collective-permute-start(bf16[2,8,8,640]{3,2,1,0:T(8,128)(2,1)} %get-tuple-element.1051), channel_id=1, source_target_pairs={{32,0},{64,32},{96,64},{128,96},{160,128},{192,160},{224,192},{33,... | collective-permute-start | bytes 491528 | tf_op jit(solution)/shard_map/while/body/eval_jaxpr/ppermute | solution.py:14
  864.6 19.4 %copy-start.78 = (f32[1,640]{1,0:T(1,128)S(1)}, f32[1,640]{1,0:T(1,128)}, u32[]{:S(2)}) copy-start(f32[1,640]{1,0:T(1,128)} %stack.274) | copy-start | bytes 7684 | tf_op jit(solution)/shard_map/while/body/eval_jaxpr/cond
  892.0 9.0 slice-start
  893.8 7.2 copy-start.6
  893.8 7.2 copy-start.8
  905.0 6.9 collective-permute-start.1
  933.7 19.4 %copy-start.78 = (f32[1,640]{1,0:T(1,128)S(1)}, f32[1,640]{1,0:T(1,128)}, u32[]{:S(2)}) copy-start(f32[1,640]{1,0:T(1,128)} %stack.274) | copy-start | bytes 7684 | tf_op jit(solution)/shard_map/while/body/eval_jaxpr/cond
  961.1 9.0 slice-start
  962.9 7.2 copy-start.6
  962.9 7.2 copy-start.8
  974.1 6.9 collective-permute-start.1
  1002.8 19.4 %copy-start.78 = (f32[1,640]{1,0:T(1,128)S(1)}, f32[1,640]{1,0:T(1,128)}, u32[]{:S(2)}) copy-start(f32[1,640]{1,0:T(1,128)} %stack.274) | copy-start | bytes 7684 | tf_op jit(solution)/shard_map/while/body/eval_jaxpr/cond
  1030.2 9.0 slice-start
  1032.0 7.2 copy-start.6
  1032.0 7.2 copy-start.8
  1043.2 6.9 collective-permute-start.1
  1071.9 19.4 %copy-start.78 = (f32[1,640]{1,0:T(1,128)S(1)}, f32[1,640]{1,0:T(1,128)}, u32[]{:S(2)}) copy-start(f32[1,640]{1,0:T(1,128)} %stack.274) | copy-start | bytes 7684 | tf_op jit(solution)/shard_map/while/body/eval_jaxpr/cond
  1099.2 9.0 slice-start
  1101.1 7.2 copy-start.8
  1112.3 6.9 collective-permute-start.1
  1121.6 59.7 %collective-permute-start.1 = (bf16[2,8,8,640]{3,2,1,0:T(8,128)(2,1)}, bf16[2,8,8,640]{3,2,1,0:T(8,128)(2,1)}, u32[]{:S(2)}, u32[]{:S(2)}) collective-permute-start(bf16[2,8,8,640]{3,2,1,0:T(8,128)(2,1)} %get-tuple-element.1051), channel_id=1, source_target_pairs={{32,0},{64,32},{96,64},{128,96},{160,128},{192,160},{224,192},{33,... | collective-permute-start | bytes 491528 | tf_op jit(solution)/shard_map/while/body/eval_jaxpr/ppermute | solution.py:14
  1275.6 130.0 %copy-start.77 = (bf16[24,2560]{1,0:T(8,128)(2,1)S(1)}, bf16[24,2560]{1,0:T(8,128)(2,1)}, u32[]{:S(2)}) copy-start(bf16[24,2560]{1,0:T(8,128)(2,1)} %fusion.2) | copy-start | bytes 368644
  1276.5 246.1 %collective-permute-start.6 = (bf16[24,2560]{1,0:T(8,128)(2,1)}, bf16[24,2560]{1,0:T(8,128)(2,1)S(1)}, u32[]{:S(2)}, u32[]{:S(2)}) collective-permute-start(bf16[24,2560]{1,0:T(8,128)(2,1)} %fusion.2), channel_id=1, source_target_pairs={{0,5},{1,6},{2,7},{3,8},{4,9},{5,10},{6,11},{7,12},{8,13},{9,14},{... | collective-permute-start | bytes 368648
  1277.8 244.8 %collective-permute-start.5 = (bf16[24,2560]{1,0:T(8,128)(2,1)}, bf16[24,2560]{1,0:T(8,128)(2,1)S(1)}, u32[]{:S(2)}, u32[]{:S(2)}) collective-permute-start(bf16[24,2560]{1,0:T(8,128)(2,1)} %fusion.2), channel_id=1, source_target_pairs={{0,4},{1,5},{2,6},{3,7},{4,8},{5,9},{6,10},{7,11},{8,12},{9,13},{1... | collective-permute-start | bytes 368648
  1279.3 243.3 %collective-permute-start.4 = (bf16[24,2560]{1,0:T(8,128)(2,1)}, bf16[24,2560]{1,0:T(8,128)(2,1)S(1)}, u32[]{:S(2)}, u32[]{:S(2)}) collective-permute-start(bf16[24,2560]{1,0:T(8,128)(2,1)} %fusion.2), channel_id=1, source_target_pairs={{0,3},{1,4},{2,5},{3,6},{4,7},{5,8},{6,9},{7,10},{8,11},{9,12},{10... | collective-permute-start | bytes 368648
  1280.6 242.0 %collective-permute-start.3 = (bf16[24,2560]{1,0:T(8,128)(2,1)}, bf16[24,2560]{1,0:T(8,128)(2,1)S(1)}, u32[]{:S(2)}, u32[]{:S(2)}) collective-permute-start(bf16[24,2560]{1,0:T(8,128)(2,1)} %fusion.2), channel_id=1, source_target_pairs={{0,2},{1,3},{2,4},{3,5},{4,6},{5,7},{6,8},{7,9},{8,10},{9,11},{10,... | collective-permute-start | bytes 368648
  1283.4 122.2 %collective-permute-start.7 = (bf16[4,2560]{1,0:T(4,128)(2,1)S(1)}, bf16[4,2560]{1,0:T(4,128)(2,1)S(1)}, u32[]{:S(2)}, u32[]{:S(2)}) collective-permute-start(bf16[4,2560]{1,0:T(4,128)(2,1)S(1)} %slice.1262), channel_id=1, source_target_pairs={{0,6},{1,7},{2,8},{3,9},{4,10},{5,11},{6,12},{7,13},{8,14},{9,15},... | collective-permute-start | bytes 61448
  1405.6 117.0 %collective-permute-start.2 = (bf16[24,2560]{1,0:T(8,128)(2,1)S(1)}, bf16[24,2560]{1,0:T(8,128)(2,1)S(1)}, u32[]{:S(2)}, u32[]{:S(2)}) collective-permute-start(bf16[24,2560]{1,0:T(8,128)(2,1)S(1)} %copy-done.77), channel_id=1, source_target_pairs={{0,1},{1,2},{2,3},{3,4},{4,5},{5,6},{6,7},{7,8},{8,9},{9,10},{10,1... | collective-permute-start | bytes 368648
  (315 other events, 698.6 us)
Sparse Core Ops, SparseCore 0:
  11.2 93.1 all-gather.4
  107.0 73.6 all-gather.6
  1186.4 193.5 reduce-scatter.3
where the time goes:
time: 1540 us; the launch traced here: 1530 us
  waiting for transfers between devices  618 us (40%)
  blocking collectives  310 us (20%)
  local copies, waits for them, and re-layouts  199 us (13%)
  starting transfers between devices  180 us (12%)
  other arithmetic  145 us (9%)
  matrix products  59.4 us (4%)
    ppermute x22, waiting for transfers between devices, from_behind(): lax.ppermute(value, axis, [(source, source + steps) for source in range(f...  453 us
    ppermute x22, starting transfers between devices, from_behind(): lax.ppermute(value, axis, [(source, source + steps) for source in range(f...  163 us
    psum x1, blocking collectives, body(): lax.psum((head_term * last_weight, loss_term * last_weight), ('section',...  116 us
    psum x1, blocking collectives, body(): lax.psum(kernel_acc.astype(jnp.bfloat16), 'dp').astype(jnp.float32)  111 us
    another operation x200, local copies, waits for them, and re-layouts, kernel_grad(): return jnp.stack(taps, axis=0)  105 us
    all_gather x1, waiting for transfers between devices, body(): lax.all_gather(weight_in[0], 'dp', axis=0, tiled=True)  91.3 us
    unnamed x1, blocking collectives  84.2 us
    all_gather x1, waiting for transfers between devices, body(): lax.all_gather(weight_out[0], 'dp', axis=0, tiled=True)  72.7 us
  transfers between devices with their start and end apart: 31, of which 24 were waited for; matrix products, arithmetic and copies ran while one was open for 8% of the time, Pallas kernels for 0%

commit v1 on v0

--- a/solution.py
+++ b/solution.py
@@ -131,8 +131,20 @@
     kernel = depth_kernels[0]
     live = jnp.arange(slot_count)[None, :] < crop_counts[0][:, None]
     entering = crop_maps[0] * live[:, :, None, None, None].astype(jnp.bfloat16)
+
+    def balance_the_points(inp):
+        return jnp.concatenate(
+            lax.all_to_all(
+                jnp.stack([inp for _ in range(lax.psum(1, axis_name="dp"))], axis=0),
+                axis_name="dp",
+                split_axis=0,
+                concat_axis=0,
+            ),
+            axis=0,
+        )
+
     first_full, second_full = (
-        lax.all_gather(weight_in[0], "dp", axis=0, tiled=True),
+        balance_the_points(weight_in[0]),
         lax.all_gather(weight_out[0], "dp", axis=0, tiled=True),
     )
     blank_tile = jnp.zeros(entering.shape[1:], jnp.bfloat16)

time: 1540 us -> 1380 us (0.90)
  waiting for transfers between devices: 618 us -> 548 us
  other arithmetic: 145 us -> 101 us
  local copies, waits for them, and re-layouts: 199 us -> 166 us
    all_to_all x0 -> x1, waiting for transfers between devices: none -> 105 us  [balance_the_points(): lax.all_to_all(jnp.stack([inp for _ in range(lax.psum(1, axis_name='dp'))...]
    all_gather x1, waiting for transfers between devices: 91.3 us -> 0.01 us  [body(): lax.all_gather(weight_in[0], 'dp', axis=0, tiled=True)]
    all_gather x1, waiting for transfers between devices: 72.7 us -> 0.01 us  [body(): lax.all_gather(weight_out[0], 'dp', axis=0, tiled=True)]
    ppermute x22, starting transfers between devices: 163 us -> 138 us  [from_behind(): lax.ppermute(value, axis, [(source, source + steps) for source in range(f...]
    dynamic_update_slice x11, other arithmetic: 19.9 us -> 1.11 us  [forward_step(): lax.dynamic_update_index_in_dim(saved, jnp.where(active, current, old_sav...]
  transfers between devices with their start and end apart: 31 -> 32, of which waited for: 24 -> 23; matrix products, arithmetic and copies ran while one was open for 8% -> 10% of each run, Pallas kernels for 0% -> 0%
where the time goes in v1:
time: 1380 us
  waiting for transfers between devices  548 us (40%)
  blocking collectives  306 us (22%)
  starting transfers between devices  169 us (12%)
  local copies, waits for them, and re-layouts  166 us (12%)
  other arithmetic  101 us (7%)
  matrix products  63.2 us (5%)
  between operations  15.3 us (1%)
    ppermute x22, waiting for transfers between devices, from_behind(): lax.ppermute(value, axis, [(source, source + steps) for source in range(f...  442 us
    ppermute x22, starting transfers between devices, from_behind(): lax.ppermute(value, axis, [(source, source + steps) for source in range(f...  138 us
    psum x1, blocking collectives, body(): lax.psum((head_term * last_weight, loss_term * last_weight), ('section',...  113 us
    psum x1, blocking collectives, body(): lax.psum(kernel_acc.astype(jnp.bfloat16), 'dp').astype(jnp.float32)  111 us
    all_to_all x1, waiting for transfers between devices, balance_the_points(): lax.all_to_all(jnp.stack([inp for _ in range(lax.psum(1, axis_name='dp'))...  105 us
    another operation x200, local copies, waits for them, and re-layouts, kernel_grad(): return jnp.stack(taps, axis=0)  105 us
    unnamed x1, blocking collectives  82.2 us
    dot_general x8, matrix products, outer_sum(): lax.dot_general(left, right, (((0,), (0,)), ((), ())), preferred_element_...  33.9 us
  transfers between devices with their start and end apart: 32, of which 23 were waited for; matrix products, arithmetic and copies ran while one was open for 10% of the time, Pallas kernels for 0%

profile of v1, /device:TPU:1, one launch (start us, length us, event | category | flops | bytes accessed | tf_op | source)
XLA Modules:
  0.0 1375.9 jit_solution(6134945424883400815)
XLA Ops:
  11.1 12.1 all-to-all-start
  24.4 105.3 %all-to-all-done = bf16[32,20,2560]{2,1,0:T(8,128)(2,1)} async-done(((bf16[32,20,2560]{2,1,0:T(8,128)(2,1)}), bf16[32,20,2560]{2,1,0:T(8,128)(2,1)}, u32[]{:S(2)}, u32[]{:S(2)}) %all-to-all-start) | async-done | bytes 3276832 | tf_op jit(solution)/shard_map/all_to_all | solution.py:137
  129.7 5.5 reshape.293
  135.4 121.2 %while.40 = (s32[]{:T(128)}, bf16[2,8,8,640]{3,2,1,0:T(8,128)(2,1)S(1)}, bf16[4,2,8,8,640]{4,3,2,1,0:T(8,128)(2,1)S(1)}, bf16[4,2,8,8,640]{4,3,2,1,0:T(8,128)(2,...) while((s32[]{:T(128)}, ...), condition=%wide.region_5.6_spmd, body=%wide.region_0.5_spmd.sunk | while | flops 849510528 | bytes 12179750 | solution.py:177
  135.6 5.5 collective-permute-start
  141.3 6.5 collective-permute-done
  147.9 7.6 conditional.5
  159.8 7.6 conditional.5
  167.3 4.4 collective-permute-start
  174.1 7.5 conditional.5
  181.6 4.4 collective-permute-start
  188.4 7.6 conditional.5
  196.0 4.4 collective-permute-start
  202.8 12.0 collective-permute-start
  217.2 4.4 collective-permute-start
  224.0 4.8 collective-permute-start
  231.2 4.4 collective-permute-start
  238.0 9.6 collective-permute-start
  250.0 4.4 collective-permute-start
  269.3 756.9 %while.41 = (s32[]{:T(128)}, bf16[2,8,8,640]{3,2,1,0:T(8,128)(2,1)}, f32[49,640]{1,0:T(8,128)S(1)}, f32[640,2560]{1,0:T(8,128)}, f32[2560,640]{1,0:T(8,128)}, /*...) while((s32[]{:T(128)}, ...), condition=%wide.region_63.64_spmd.clone, body=%wide.region_7.63_spmd.clone.sunk | while | flops 2131804288 | bytes 130983528 | solution.py:224
  273.6 6.2 collective-permute-done.1
  284.1 5.0 collective-permute-done.1
  293.4 10.7 collective-permute-done.1
  308.4 5.0 collective-permute-done.1
  317.7 6.1 collective-permute-done.1
  328.1 359.6 %collective-permute-done.1 = bf16[2,8,8,640]{3,2,1,0:T(8,128)(2,1)} collective-permute-done((bf16[2,8,8,640]{3,2,1,0:T(8,128)(2,1)}, bf16[2,8,8,640]{3,2,1,0:T(8,128)(2,1)}, u32[]{:S(2)}, u32[]{:S(2)}) %collective-permute-start.1) | collective-permute-done | bytes 163872 | tf_op jit(solution)/shard_map/while/body/eval_jaxpr/ppermute | solution.py:14
  689.4 60.5 %conditional.6 = (bf16[2,8,8,640]{3,2,1,0:T(8,128)(2,1)}, f32[49,640]{1,0:T(8,128)S(1)}, f32[640,2560]{1,0:T(8,128)}, f32[2560,640]{1,0:T(8,128)}) conditional(s32[]{:T(128)} %convert_element_type.175, (f32[49,640]{1,0:T(8,128)S(1)}, f32[640,2560]{1,0:T(8,128)}, f32[2560,640]{1,0:T(8,128)}) %tuple.251, (pred[]{:T(512)}, s32[]{:T(128)}, ...), branch_computations={%region_8.8_spmd, %region_9.62_spmd} | conditional | flops 2131148928 | bytes 129667864 | solution.py:218
  728.9 8.0 stack.301
  738.6 7.2 convolution_add_fusion.1
  751.8 5.0 collective-permute-done.1
  758.5 60.5 %conditional.6 = (bf16[2,8,8,640]{3,2,1,0:T(8,128)(2,1)}, f32[49,640]{1,0:T(8,128)S(1)}, f32[640,2560]{1,0:T(8,128)}, f32[2560,640]{1,0:T(8,128)}) conditional(s32[]{:T(128)} %convert_element_type.175, (f32[49,640]{1,0:T(8,128)S(1)}, f32[640,2560]{1,0:T(8,128)}, f32[2560,640]{1,0:T(8,128)}) %tuple.251, (pred[]{:T(512)}, s32[]{:T(128)}, ...), branch_computations={%region_8.8_spmd, %region_9.62_spmd} | conditional | flops 2131148928 | bytes 129667864 | solution.py:218
  797.9 8.0 stack.301
  807.7 7.2 convolution_add_fusion.1
  820.9 5.0 collective-permute-done.1
  827.6 60.5 %conditional.6 = (bf16[2,8,8,640]{3,2,1,0:T(8,128)(2,1)}, f32[49,640]{1,0:T(8,128)S(1)}, f32[640,2560]{1,0:T(8,128)}, f32[2560,640]{1,0:T(8,128)}) conditional(s32[]{:T(128)} %convert_element_type.175, (f32[49,640]{1,0:T(8,128)S(1)}, f32[640,2560]{1,0:T(8,128)}, f32[2560,640]{1,0:T(8,128)}) %tuple.251, (pred[]{:T(512)}, s32[]{:T(128)}, ...), branch_computations={%region_8.8_spmd, %region_9.62_spmd} | conditional | flops 2131148928 | bytes 129667864 | solution.py:218
  867.0 8.0 stack.301
  876.8 7.2 convolution_add_fusion.1
  890.0 5.0 collective-permute-done.1
  896.7 60.5 %conditional.6 = (bf16[2,8,8,640]{3,2,1,0:T(8,128)(2,1)}, f32[49,640]{1,0:T(8,128)S(1)}, f32[640,2560]{1,0:T(8,128)}, f32[2560,640]{1,0:T(8,128)}) conditional(s32[]{:T(128)} %convert_element_type.175, (f32[49,640]{1,0:T(8,128)S(1)}, f32[640,2560]{1,0:T(8,128)}, f32[2560,640]{1,0:T(8,128)}) %tuple.251, (pred[]{:T(512)}, s32[]{:T(128)}, ...), branch_computations={%region_8.8_spmd, %region_9.62_spmd} | conditional | flops 2131148928 | bytes 129667864 | solution.py:218
  936.1 8.0 stack.301
  945.9 7.2 convolution_add_fusion.1
  959.1 5.0 collective-permute-done.1
  966.5 58.4 %collective-permute-start.1 = (bf16[2,8,8,640]{3,2,1,0:T(8,128)(2,1)}, bf16[2,8,8,640]{3,2,1,0:T(8,128)(2,1)}, u32[]{:S(2)}, u32[]{:S(2)}) collective-permute-start(bf16[2,8,8,640]{3,2,1,0:T(8,128)(2,1)} %get-tuple-element.1051), channel_id=1, source_target_pairs={{32,0},{64,32},{96,64},{128,96},{160,128},{192,160},{224,192},{33,... | collective-permute-start | bytes 491528 | tf_op jit(solution)/shard_map/while/body/eval_jaxpr/ppermute | solution.py:14
  1026.2 4.9 convert_element_type.134
  1036.2 82.2 %fusion.2 = bf16[24,2560]{1,0:T(8,128)(2,1)} fusion(bf16[640,2560]{1,0:T(8,128)(2,1)S(1)} %convert_element_type.133), kind=kCustom, calls=%all-reduce-scatter | all-reduce-scatter fusion | flops 1966081 | bytes 3400704
  1127.0 11.3 collective-permute-start.7
  1139.6 110.7 %psum.21 = bf16[1,49,640]{2,0,1:T(2,128)(2,1)S(1)} all-reduce(bf16[1,49,640]{2,0,1:T(2,128)(2,1)S(1)} %broadcast_in_dim.64), channel_id=1, replica_groups=mesh['section'=8,'dp'=32] {'dp'}, use_global_device_ids=true, to_apply=%region_66.67 | all-reduce | flops 31360 | bytes 125440 | tf_op jit(solution)/shard_map/psum | solution.py:235
  1252.4 113.0 %all-reduce.5 = (f32[640]{0:T(1024)}, f32[]{:T(128)}) all-reduce(f32[640]{0:T(1024)S(1)} %broadcast_multiply_fusion.4, f32[]{:T(128)S(6)} %mul.2377), channel_id=1, replica_groups=mesh['section'=8,'dp'=32] {'section','dp'}, use_global_device_ids=true, to_apply=%region_68.69 | all-reduce | flops 641 | bytes 5128 | tf_op jit(solution)/shard_map/psum | solution.py:184
  (1160 shorter events, 318.1 us)
Async XLA Ops:
  7.2 128.1 %all-gather.5.cloned.1.call-start = ((), (), s32[]{:S(2)}) async-start(), calls=%async_computation.3 | async-start | bytes 3379200 | tf_op jit(solution)/shard_map/all_gather | solution.py:148
  11.0 12.2 copy-start.80
  11.0 13.1 copy-start.84
  11.0 13.1 copy-start.86
  11.0 13.2 copy-start.78
  11.1 118.7 %all-to-all-start = ((bf16[32,20,2560]{2,1,0:T(8,128)(2,1)}), bf16[32,20,2560]{2,1,0:T(8,128)(2,1)}, u32[]{:S(2)}, u32[]{:S(2)}) async-start(bf16[32,20,2560]{2,1,0:T(8,128)(2,1)} %stack.303), calls=%async_computation | async-start | bytes 7864320 | tf_op jit(solution)/shard_map/all_to_all | solution.py:137
  23.2 235.1 %all-gather.7.cloned.1.call-start = ((), (), s32[]{:S(2)}) async-start(), calls=%async_computation.4 | async-start | bytes 6758400 | tf_op jit(solution)/shard_map/all_gather | solution.py:188
  24.1 1343.7 %reduce-scatter.4.cloned.1.call-start = ((), (), s32[]{:S(2)}) async-start(), calls=%async_computation.2 | async-start | bytes 3379200 | tf_op jit(solution)/shard_map/reduce_scatter | solution.py:231
  135.4 122.2 %copy-start.85 = (s32[1,4,2,8,8]{4,3,2,1,0:T(8,128)S(1)}, s32[1,4,2,8,8]{4,3,2,1,0:T(8,128)}, u32[]{:S(2)}) copy-start(s32[1,4,2,8,8]{4,3,2,1,0:T(8,128)} %param.16) | copy-start | bytes 6148
  135.6 12.1 collective-permute-start
  155.5 4.2 collective-permute-start
  167.3 6.6 collective-permute-start
  181.6 6.6 collective-permute-start
  196.0 6.7 collective-permute-start
  202.8 14.2 %collective-permute-start = (bf16[2,8,8,640]{3,2,1,0:T(8,128)(2,1)S(1)}, bf16[2,8,8,640]{3,2,1,0:T(8,128)(2,1)S(1)}, u32[]{:S(2)}, u32[]{:S(2)}) collective-permute-start(bf16[2,8,8,640]{3,2,1,0:T(8,128)(2,1)S(1)} %get-tuple-element.1153), channel_id=1, source_target_pairs={{0,32},{32,64},{64,96},{96,128},{128,160},{160,192},{192,224},{1,3... | collective-permute-start | bytes 491528 | tf_op jit(solution)/shard_map/while/body/eval_jaxpr/ppermute | solution.py:14
  217.2 6.6 collective-permute-start
  224.0 7.1 collective-permute-start
  231.2 6.6 collective-permute-start
  238.0 11.8 collective-permute-start
  250.0 6.6 collective-permute-start
  271.7 8.1 collective-permute-start.1
  282.2 6.9 collective-permute-start.1
  291.5 12.6 collective-permute-start.1
  306.5 6.9 collective-permute-start.1
  315.8 8.0 collective-permute-start.1
  326.2 361.5 %collective-permute-start.1 = (bf16[2,8,8,640]{3,2,1,0:T(8,128)(2,1)}, bf16[2,8,8,640]{3,2,1,0:T(8,128)(2,1)}, u32[]{:S(2)}, u32[]{:S(2)}) collective-permute-start(bf16[2,8,8,640]{3,2,1,0:T(8,128)(2,1)} %get-tuple-element.1051), channel_id=1, source_target_pairs={{32,0},{64,32},{96,64},{128,96},{160,128},{192,160},{224,192},{33,... | collective-permute-start | bytes 491528 | tf_op jit(solution)/shard_map/while/body/eval_jaxpr/ppermute | solution.py:14
  709.4 19.4 %copy-start.81 = (f32[1,640]{1,0:T(1,128)S(1)}, f32[1,640]{1,0:T(1,128)}, u32[]{:S(2)}) copy-start(f32[1,640]{1,0:T(1,128)} %stack.276) | copy-start | bytes 7684 | tf_op jit(solution)/shard_map/while/body/eval_jaxpr/cond
  736.8 9.0 slice-start
  738.6 7.2 copy-start.8
  749.9 6.9 collective-permute-start.1
  778.5 19.4 %copy-start.81 = (f32[1,640]{1,0:T(1,128)S(1)}, f32[1,640]{1,0:T(1,128)}, u32[]{:S(2)}) copy-start(f32[1,640]{1,0:T(1,128)} %stack.276) | copy-start | bytes 7684 | tf_op jit(solution)/shard_map/while/body/eval_jaxpr/cond
  805.9 9.0 slice-start
  807.7 7.2 copy-start.8
  819.0 6.9 collective-permute-start.1
  847.6 19.4 %copy-start.81 = (f32[1,640]{1,0:T(1,128)S(1)}, f32[1,640]{1,0:T(1,128)}, u32[]{:S(2)}) copy-start(f32[1,640]{1,0:T(1,128)} %stack.276) | copy-start | bytes 7684 | tf_op jit(solution)/shard_map/while/body/eval_jaxpr/cond
  875.0 9.0 slice-start
  888.1 6.9 collective-permute-start.1
  916.7 19.4 %copy-start.81 = (f32[1,640]{1,0:T(1,128)S(1)}, f32[1,640]{1,0:T(1,128)}, u32[]{:S(2)}) copy-start(f32[1,640]{1,0:T(1,128)} %stack.276) | copy-start | bytes 7684 | tf_op jit(solution)/shard_map/while/body/eval_jaxpr/cond
  944.1 9.0 slice-start
  957.2 6.9 collective-permute-start.1
  966.5 59.7 %collective-permute-start.1 = (bf16[2,8,8,640]{3,2,1,0:T(8,128)(2,1)}, bf16[2,8,8,640]{3,2,1,0:T(8,128)(2,1)}, u32[]{:S(2)}, u32[]{:S(2)}) collective-permute-start(bf16[2,8,8,640]{3,2,1,0:T(8,128)(2,1)} %get-tuple-element.1051), channel_id=1, source_target_pairs={{32,0},{64,32},{96,64},{128,96},{160,128},{192,160},{224,192},{33,... | collective-permute-start | bytes 491528 | tf_op jit(solution)/shard_map/while/body/eval_jaxpr/ppermute | solution.py:14
  1118.4 132.7 %copy-start.79 = (bf16[24,2560]{1,0:T(8,128)(2,1)S(1)}, bf16[24,2560]{1,0:T(8,128)(2,1)}, u32[]{:S(2)}) copy-start(bf16[24,2560]{1,0:T(8,128)(2,1)} %fusion.2) | copy-start | bytes 368644
  1119.3 246.2 %collective-permute-start.6 = (bf16[24,2560]{1,0:T(8,128)(2,1)}, bf16[24,2560]{1,0:T(8,128)(2,1)S(1)}, u32[]{:S(2)}, u32[]{:S(2)}) collective-permute-start(bf16[24,2560]{1,0:T(8,128)(2,1)} %fusion.2), channel_id=1, source_target_pairs={{0,5},{1,6},{2,7},{3,8},{4,9},{5,10},{6,11},{7,12},{8,13},{9,14},{... | collective-permute-start | bytes 368648
  1120.6 244.9 %collective-permute-start.5 = (bf16[24,2560]{1,0:T(8,128)(2,1)}, bf16[24,2560]{1,0:T(8,128)(2,1)S(1)}, u32[]{:S(2)}, u32[]{:S(2)}) collective-permute-start(bf16[24,2560]{1,0:T(8,128)(2,1)} %fusion.2), channel_id=1, source_target_pairs={{0,4},{1,5},{2,6},{3,7},{4,8},{5,9},{6,10},{7,11},{8,12},{9,13},{1... | collective-permute-start | bytes 368648
  1122.1 243.3 %collective-permute-start.4 = (bf16[24,2560]{1,0:T(8,128)(2,1)}, bf16[24,2560]{1,0:T(8,128)(2,1)S(1)}, u32[]{:S(2)}, u32[]{:S(2)}) collective-permute-start(bf16[24,2560]{1,0:T(8,128)(2,1)} %fusion.2), channel_id=1, source_target_pairs={{0,3},{1,4},{2,5},{3,6},{4,7},{5,8},{6,9},{7,10},{8,11},{9,12},{10... | collective-permute-start | bytes 368648
  1123.4 242.0 %collective-permute-start.3 = (bf16[24,2560]{1,0:T(8,128)(2,1)}, bf16[24,2560]{1,0:T(8,128)(2,1)S(1)}, u32[]{:S(2)}, u32[]{:S(2)}) collective-permute-start(bf16[24,2560]{1,0:T(8,128)(2,1)} %fusion.2), channel_id=1, source_target_pairs={{0,2},{1,3},{2,4},{3,5},{4,6},{5,7},{6,8},{7,9},{8,10},{9,11},{10,... | collective-permute-start | bytes 368648
  1127.0 124.1 %collective-permute-start.7 = (bf16[4,2560]{1,0:T(4,128)(2,1)S(1)}, bf16[4,2560]{1,0:T(4,128)(2,1)S(1)}, u32[]{:S(2)}, u32[]{:S(2)}) collective-permute-start(bf16[4,2560]{1,0:T(4,128)(2,1)S(1)} %slice.1262), channel_id=1, source_target_pairs={{0,6},{1,7},{2,8},{3,9},{4,10},{5,11},{6,12},{7,13},{8,14},{9,15},... | collective-permute-start | bytes 61448
  1251.1 114.4 %collective-permute-start.2 = (bf16[24,2560]{1,0:T(8,128)(2,1)S(1)}, bf16[24,2560]{1,0:T(8,128)(2,1)S(1)}, u32[]{:S(2)}, u32[]{:S(2)}) collective-permute-start(bf16[24,2560]{1,0:T(8,128)(2,1)S(1)} %copy-done.79), channel_id=1, source_target_pairs={{0,1},{1,2},{2,3},{3,4},{4,5},{5,6},{6,7},{7,8},{8,9},{9,10},{10,1... | collective-permute-start | bytes 368648
  (318 other events, 732.6 us)
Sparse Core Ops, SparseCore 0:
  10.6 117.2 all-gather.4
  131.0 91.5 all-gather.6
  1031.2 194.6 reduce-scatter.3
